TPU v7x, 32 devices: a whole 2x2x4 slice. The times are simulated.
32 devices in a mesh: grp: 2 (over x), ctx: 16 (over z, y, core).
Axes of the slice: x: 2, y: 2, z: 4, core: 2. Of those that a mesh axis runs over, the one named last changes fastest.
Arguments:
- queries: bfloat16 [2, 24, 64, 576], P('grp', None, 'ctx'), parts along dimension 0, may hold values from -40 to 40
- cache: bfloat16 [2, 8192, 576], P('grp', 'ctx'), parts along dimension 0, may hold values from -6 to 6
- draft_latent: bfloat16 [2, 24, 576], P('grp'), parts along dimension 0, may hold values from -9 to 9
- lengths: int32 [2], P('grp'), parts along dimension 0, may hold values from 4096 to 8192
- parents: int32 [2, 24], P('grp'), parts along dimension 0, may hold values from -1 to 22, as said below
- value_up: bfloat16 [64, 512, 128], P('ctx'), may hold values from -0.25 to 0.25
- out_proj: bfloat16 [8192, 7168], P('ctx'), may hold values from -0.09375 to 0.09375
Outputs:
- attended: bfloat16 [48, 7168], P('grp', 'ctx'), parts along dimension 0
There are 2 independent parts, one for each index of `grp`. A program takes and returns all parts, laid end to end along the dimension named above; an argument that names none is the same for every part. Nothing has to cross between parts.
Inputs may be any that keep to these rules, and one draw needn't show every extreme that they name: parents[r, 0] = -1 and 0 <= parents[r, i] < i for i >= 1.
All inputs are finite; a program needn't handle non-finite values.
Results may differ from a plain program's by a relative error of at most 0.007.
Values may be sent and summed in bfloat16 or wider, within the bound.
A program may use at most 64 MiB of HBM per device.

v0:
```python
import math
import jax
import jax.numpy as jnp
from jax import lax
from jax.sharding import PartitionSpec as P

yarn_factor = 1.0 + 0.1 * math.log(32.0)
score_scale = yarn_factor * yarn_factor / math.sqrt(192.0)
neg_fill = -1e30


def tree_reach(parents):
    drafts = parents.shape[1]
    order = jnp.arange(drafts, dtype=jnp.int32)
    adjacent = (parents[:, :, None] == order[None, None, :]).astype(jnp.float32)
    ident = jnp.broadcast_to(jnp.eye(drafts, dtype=jnp.float32), adjacent.shape)

    def extend(step, reach):
        grown = ident + jnp.einsum("rij,rjk->rik", adjacent, reach, precision=lax.Precision.HIGHEST)
        return jnp.minimum(grown, 1.0)

    return lax.fori_loop(0, drafts, extend, ident) > 0.5


def block_state(rows, keys, valid, latent_width):
    scores = (
        lax.dot_general(
            rows, keys, (((2,), (2,)), ((0,), (0,))), preferred_element_type=jnp.float32
        )
        * score_scale
    )
    masked = jnp.where(valid, scores, neg_fill)
    top = jnp.max(masked, axis=2)
    weights = jnp.where(valid, jnp.exp(masked - top[:, :, None]), 0.0).astype(jnp.bfloat16)
    numer = lax.dot_general(
        weights, keys, (((2,), (1,)), ((0,), (0,))), preferred_element_type=jnp.float32
    )
    total = jnp.sum(weights.astype(jnp.float32), axis=2)
    return (numer[:, :, :latent_width], top, total)


def join(first, second):
    best = jnp.maximum(first[1], second[1])
    factor_a = jnp.exp(first[1] - best)
    factor_b = jnp.exp(second[1] - best)
    return (
        first[0] * factor_a[..., None] + second[0] * factor_b[..., None],
        best,
        first[2] * factor_a + second[2] * factor_b,
    )


def on_device(queries, cache, draft_latent, lengths, parents, value_up, out_proj):
    requests, drafts, heads_here, width = queries.shape
    block_len = cache.shape[1]
    latent_width = value_up.shape[1]
    myself = lax.axis_index("ctx")
    positions = myself * block_len + jnp.arange(block_len, dtype=jnp.int32)
    live = (positions[None, :] < lengths[:, None])[:, None, :]
    own_rows = queries.reshape(requests, drafts * heads_here, width)
    every = lax.all_gather(queries, "ctx", axis=2, tiled=True)
    heads = every.shape[2]
    rows = every.reshape(requests, drafts * heads, width)
    numer, top, total = block_state(rows, cache, live, latent_width)
    numer = numer.reshape(1, requests, drafts, heads, latent_width)
    top = top.reshape(1, requests, drafts, heads)
    total = total.reshape(1, requests, drafts, heads)
    numers, tops, totals = (
        lax.all_to_all(numer, "ctx", split_axis=3, concat_axis=0, tiled=True),
        lax.all_to_all(top, "ctx", split_axis=3, concat_axis=0, tiled=True),
        lax.all_to_all(total, "ctx", split_axis=3, concat_axis=0, tiled=True),
    )
    best = jnp.max(tops, axis=0)
    factor = jnp.exp(tops - best[None])
    context = (
        jnp.sum(numers * factor[..., None], axis=0).reshape(
            requests, drafts * heads_here, latent_width
        ),
        best.reshape(requests, drafts * heads_here),
        jnp.sum(totals * factor, axis=0).reshape(requests, drafts * heads_here),
    )
    reach = tree_reach(parents)
    tree = jnp.repeat(reach, heads_here, axis=1)
    whole = join(context, block_state(own_rows, draft_latent, tree, latent_width))
    latent_out = (whole[0] / whole[2][..., None]).astype(jnp.bfloat16)
    latent_out = latent_out.reshape(requests, drafts, heads_here, latent_width)
    values = jnp.einsum(
        "rdhl,hlv->rdhv", latent_out, value_up, preferred_element_type=jnp.float32
    ).astype(jnp.bfloat16)
    flat = values.reshape(requests * drafts, heads_here * value_up.shape[2])
    partial_value = jnp.dot(flat, out_proj, preferred_element_type=jnp.float32)
    return lax.psum_scatter(partial_value, "ctx", scatter_dimension=1, tiled=True).astype(
        jnp.bfloat16
    )


def solution(mesh):
    in_specs = (
        P("grp", None, "ctx", None),
        P("grp", "ctx", None),
        P("grp", None, None),
        P("grp"),
        P("grp", None),
        P("ctx", None, None),
        P("ctx", None),
    )
    out_specs = P("grp", "ctx")
    return jax.shard_map(
        on_device, mesh=mesh, in_specs=in_specs, out_specs=out_specs, check_vma=False
    )
```

profile of v0, /device:TPU:0, one launch (start us, length us, event | category | flops | bytes accessed | tf_op | source)
XLA Modules:
  0.0 251.4 jit_solution(7607140488094526132)
XLA Ops:
  6.5 1.6 copy.40
  8.9 44.5 %all-gather.2.cloned.1.call-done = bf16[1,24,64,576]{3,1,0,2:T(8,128)(2,1)} async-done(((bf16[1,24,4,576]{3,1,0,2:T(8,128)(2,1)}), bf16[1,24,64,576]{3,1,0,2:T(8,128)(2,1)}) %all-gather.2.cloned.1.call-update) | async-done | bytes 1769488 | tf_op jit(solution)/shard_map/all_gather | solution.py:61
  53.4 1.9 copy.41
  55.3 1.5 fusion.29
  56.8 1.7 copy-done.1
  58.5 0.6 convert_reduce_fusion
  59.1 0.7 copy.49
  59.8 3.5 %all-to-all-start.2 = ((f32[1,1,24,64]{2,1,0,3:T(1,128)}), f32[1,1,24,64]{2,1,0,3:T(1,128)S(1)}, u32[]{:S(2)}, u32[]{:S(2)}) async-start(f32[1,1,24,64]{2,1,0,3:T(1,128)} %copy.49), calls=%async_computation.2 | async-start | bytes 65536 | tf_op jit(solution)/shard_map/all_to_all | solution.py:71
  63.4 0.7 copy.44
  64.1 5.9 %all-to-all-done.2 = f32[1,1,24,64]{2,1,0,3:T(1,128)S(1)} async-done(((f32[1,1,24,64]{2,1,0,3:T(1,128)}), f32[1,1,24,64]{2,1,0,3:T(1,128)S(1)}, u32[]{:S(2)}, u32[]{:S(2)}) %all-to-all-start.2) | async-done | bytes 6176 | tf_op jit(solution)/shard_map/all_to_all | solution.py:71
  69.9 3.5 %all-to-all-start.1 = ((f32[1,1,24,64]{2,1,0,3:T(1,128)}), f32[1,1,24,64]{2,1,0,3:T(1,128)S(1)}, u32[]{:S(2)}, u32[]{:S(2)}) async-start(f32[1,1,24,64]{2,1,0,3:T(1,128)} %copy.44), calls=%async_computation.1 | async-start | bytes 65536 | tf_op jit(solution)/shard_map/all_to_all | solution.py:70
  73.4 3.1 %convolution_bitcast_fusion.1 = f32[1,1536,576]{1,2,0:T(8,128)S(1)} fusion(bf16[1,512,576]{1,2,0:T(8,128)(2,1)S(1)} %copy-done, f32[1536,512]{0,1:T(8,128)} %copy-done.1, f32[1536]{0:T(1024)S(1)} %get-tuple-element.49, pred[512]{0:T(512)(128)(4,1)S(1)} %add_compare_fusion), kind=kOutput, calls=%fused_computation.12 | convolution fusion | flops 908328960 | bytes 7281152 | tf_op jit(solution)/shard_map/dot_general | solution.py:35
  76.5 1.9 slice.8
  78.4 3.6 %copy.42 = f32[1,1536,512]{2,1,0:T(8,128)} copy(f32[1,1536,512]{1,2,0:T(8,128)} %slice.8) | data formatting | bytes 6291456 | tf_op jit(solution)/shard_map/slice | solution.py:39
  82.0 5.4 %copy.43 = f32[1,1,24,64,512]{4,2,1,0,3:T(8,128)} copy(f32[1,1,24,64,512]{4,3,2,1,0:T(8,128)} %bitcast.82) | data formatting | bytes 6291456 | tf_op jit(solution)/shard_map/reshape | solution.py:65
  87.4 6.2 %all-to-all-start = ((f32[1,1,24,64,512]{4,2,1,0,3:T(8,128)}), f32[1,1,24,64,512]{4,2,1,0,3:T(8,128)}, u32[]{:S(2)}, u32[]{:S(2)}) async-start(f32[1,1,24,64,512]{4,2,1,0,3:T(8,128)} %copy.43), calls=%async_computation | async-start | bytes 6291456 | tf_op jit(solution)/shard_map/all_to_all | solution.py:69
  93.7 5.8 %while.11 = (s32[]{:T(128)}, f32[1,24,24]{2,1,0:T(8,128)S(1)}, s32[24]{0:T(128)S(1)}, s32[]{:T(128)}) while((s32[]{:T(128)}, f32[1,24,24]{2,1,0:T(8,128)S(1)}, s32[24]{0:T(128)S(1)}, s32[]{:T(128)}) %tuple.32), condition=%wide.region_4.5_spmd.clone, body=%wide.region_3.4_spmd.clone.sunk | while | flops 169346 | bytes 9365 | solution.py:22
  93.7 0.2 fusion.39
  99.9 0.2 convolution_bitcast_fusion.2
  100.6 52.2 %all-to-all-done = f32[1,1,24,64,512]{4,2,1,0,3:T(8,128)} async-done(((f32[1,1,24,64,512]{4,2,1,0,3:T(8,128)}), f32[1,1,24,64,512]{4,2,1,0,3:T(8,128)}, u32[]{:S(2)}, u32[]{:S(2)}) %all-to-all-start) | async-done | bytes 3145760 | tf_op jit(solution)/shard_map/all_to_all | solution.py:69
  152.8 2.2 multiply_reduce_fusion
  155.6 7.8 %convolution_bitcast_fusion = f32[7168,24]{1,0:T(8,128)} fusion(bf16[512,7168]{1,0:T(8,128)(2,1)} %param.15, bf16[3,8,4,128]{3,2,1,0:T(4,128)(2,1)S(1)} %bitcast.90), kind=kOutput, calls=%fused_computation.11 | convolution fusion | flops 176160768 | bytes 8052736
  163.5 79.5 %reduce-scatter.4.cloned.1.call-done = f32[448,24]{1,0:T(8,128)} async-done(((f32[7168,24]{1,0:T(8,128)}), f32[448,24]{1,0:T(8,128)}) %reduce-scatter.4.cloned.1.call-update) | async-done | bytes 43024
  243.0 1.6 copy.54
  (88 shorter events, 6.5 us)
Async XLA Ops:
  6.5 48.7 %copy-start = (bf16[1,512,576]{1,2,0:T(8,128)(2,1)S(1)}, bf16[1,512,576]{1,2,0:T(8,128)(2,1)}, u32[]{:S(2)}) copy-start(bf16[1,512,576]{1,2,0:T(8,128)(2,1)} %param.10) | copy-start | bytes 1769476
  6.5 46.9 %all-gather.2.cloned.1.call-start = ((), (), s32[]{:S(2)}) async-start(), calls=%async_computation.4 | async-start | bytes 2088960 | tf_op jit(solution)/shard_map/all_gather | solution.py:61
  56.8 1.7 copy-start.1
  59.8 10.1 %all-to-all-start.2 = ((f32[1,1,24,64]{2,1,0,3:T(1,128)}), f32[1,1,24,64]{2,1,0,3:T(1,128)S(1)}, u32[]{:S(2)}, u32[]{:S(2)}) async-start(f32[1,1,24,64]{2,1,0,3:T(1,128)} %copy.49), calls=%async_computation.2 | async-start | bytes 65536 | tf_op jit(solution)/shard_map/all_to_all | solution.py:71
  69.9 17.4 %all-to-all-start.1 = ((f32[1,1,24,64]{2,1,0,3:T(1,128)}), f32[1,1,24,64]{2,1,0,3:T(1,128)S(1)}, u32[]{:S(2)}, u32[]{:S(2)}) async-start(f32[1,1,24,64]{2,1,0,3:T(1,128)} %copy.44), calls=%async_computation.1 | async-start | bytes 65536 | tf_op jit(solution)/shard_map/all_to_all | solution.py:70
  87.3 6.2 %copy-start.3 = (bf16[1,24,4,576]{3,2,1,0:T(4,128)(2,1)S(1)}, bf16[1,24,4,576]{3,2,1,0:T(4,128)(2,1)}, u32[]{:S(2)}) copy-start(bf16[1,24,4,576]{3,2,1,0:T(4,128)(2,1)} %param.9) | copy-start | bytes 331780
  87.4 6.3 %copy-start.5 = (s32[1,24]{1,0:T(1,128)S(1)}, s32[1,24]{1,0:T(1,128)}, u32[]{:S(2)}) copy-start(s32[1,24]{1,0:T(1,128)} %param.13) | copy-start | bytes 292
  87.4 12.3 %copy-start.4 = (bf16[1,24,576]{2,1,0:T(8,128)(2,1)S(1)}, bf16[1,24,576]{2,1,0:T(8,128)(2,1)}, u32[]{:S(2)}) copy-start(bf16[1,24,576]{2,1,0:T(8,128)(2,1)} %param.11) | copy-start | bytes 82948
  87.4 65.5 %all-to-all-start = ((f32[1,1,24,64,512]{4,2,1,0,3:T(8,128)}), f32[1,1,24,64,512]{4,2,1,0,3:T(8,128)}, u32[]{:S(2)}, u32[]{:S(2)}) async-start(f32[1,1,24,64,512]{4,2,1,0,3:T(8,128)} %copy.43), calls=%async_computation | async-start | bytes 6291456 | tf_op jit(solution)/shard_map/all_to_all | solution.py:69
  93.5 149.4 %reduce-scatter.4.cloned.1.call-start = ((), (), s32[]{:S(2)}) async-start(), calls=%async_computation.5 | async-start | bytes 3899392
  93.7 61.7 %copy-start.2 = (bf16[4,512,128]{2,1,0:T(8,128)(2,1)S(1)}, bf16[4,512,128]{2,1,0:T(8,128)(2,1)}, u32[]{:S(2)}) copy-start(bf16[4,512,128]{2,1,0:T(8,128)(2,1)} %param.14) | copy-start | bytes 1572868
Sparse Core Ops, SparseCore 0:
  9.6 43.7 all-gather.1
  163.6 79.3 reduce-scatter.3
where the time goes:
time: 252 us; the launch traced here: 251 us
  waiting for transfers between devices  182 us (72%)
  local copies, waits for them, and re-layouts  20 us (8%)
  matrix products  18 us (7%)
  between operations  14.3 us (6%)
  starting transfers between devices  13.2 us (5%)
  other arithmetic  2.99 us (1%)
    unnamed x3, waiting for transfers between devices  79.5 us
    all_to_all x1, waiting for transfers between devices, on_device(): lax.all_to_all(numer, 'ctx', split_axis=3, concat_axis=0, tiled=True)  52.2 us
    all_gather x1, waiting for transfers between devices, on_device(): every = lax.all_gather(queries, 'ctx', axis=2, tiled=True)  44.5 us
    unnamed x1, matrix products  7.84 us
    all_to_all x1, starting transfers between devices, on_device(): lax.all_to_all(numer, 'ctx', split_axis=3, concat_axis=0, tiled=True)  6.16 us
    all_to_all x1, waiting for transfers between devices, on_device(): lax.all_to_all(total, 'ctx', split_axis=3, concat_axis=0, tiled=True)  5.86 us
    slice x2, local copies, waits for them, and re-layouts, block_state(): return (numer[:, :, :latent_width], top, total)  5.45 us
    reshape x1, local copies, waits for them, and re-layouts, on_device(): numer = numer.reshape(1, requests, drafts, heads, latent_width)  5.38 us
  transfers between devices with their start and end apart: 5, of which 4 were waited for; matrix products, arithmetic and copies ran while one was open for 8% of the time, Pallas kernels for 0%

commit v1 on v0

--- a/solution.py
+++ b/solution.py
@@ -65,8 +65,18 @@
     numer = numer.reshape(1, requests, drafts, heads, latent_width)
     top = top.reshape(1, requests, drafts, heads)
     total = total.reshape(1, requests, drafts, heads)
+
+    def prepare_wall_all(inner_x, a_name, array_axis, on_dim):
+        b_next = jnp.concatenate(
+            lax.all_to_all(
+                jnp.stack(jnp.split(inner_x, lax.psum(1, a_name), array_axis), 0), a_name, 0, 0
+            ),
+            on_dim,
+        )
+        return b_next
+
     numers, tops, totals = (
-        lax.all_to_all(numer, "ctx", split_axis=3, concat_axis=0, tiled=True),
+        prepare_wall_all(numer, "ctx", 3, 0),
         lax.all_to_all(top, "ctx", split_axis=3, concat_axis=0, tiled=True),
         lax.all_to_all(total, "ctx", split_axis=3, concat_axis=0, tiled=True),
     )

time: 252 us -> 278 us (1.10)
  local copies, waits for them, and re-layouts: 20 us -> 42.4 us
    unnamed x15 -> x30, local copies, waits for them, and re-layouts: 4.94 us -> 29.1 us
    reshape x1 -> x0, local copies, waits for them, and re-layouts: 5.38 us -> none  [on_device(): numer = numer.reshape(1, requests, drafts, heads, latent_width)]
  transfers between devices with their start and end apart: 5 -> 5, of which waited for: 4 -> 4; matrix products, arithmetic and copies ran while one was open for 8% -> 15% of each run, Pallas kernels for 0% -> 0%
where the time goes in v1:
time: 278 us; the launch traced here: 277 us
  waiting for transfers between devices  181 us (65%)
  local copies, waits for them, and re-layouts  42.4 us (15%)
  matrix products  19.6 us (7%)
  between operations  14.3 us (5%)
  starting transfers between devices  14 us (5%)
  other arithmetic  5.16 us (2%)
    unnamed x3, waiting for transfers between devices  79.4 us
    all_to_all x1, waiting for transfers between devices, prepare_wall_all(): lax.all_to_all(jnp.stack(jnp.split(inner_x, lax.psum(1, a_name), array_ax...  52 us
    all_gather x1, waiting for transfers between devices, on_device(): every = lax.all_gather(queries, 'ctx', axis=2, tiled=True)  44.5 us
    unnamed x30, local copies, waits for them, and re-layouts  29.1 us
    unnamed x1, matrix products  7.84 us
    slice x2, local copies, waits for them, and re-layouts, block_state(): return (numer[:, :, :latent_width], top, total)  7.31 us
    all_to_all x1, starting transfers between devices, on_device(): lax.all_to_all(total, 'ctx', split_axis=3, concat_axis=0, tiled=True)  5.99 us
  transfers between devices with their start and end apart: 5, of which 4 were waited for; matrix products, arithmetic and copies ran while one was open for 15% of the time, Pallas kernels for 0%

profile of v1, /device:TPU:0, one launch (start us, length us, event | category | flops | bytes accessed | tf_op | source)
XLA Modules:
  0.0 277.1 jit_solution(878397136023374847)
XLA Ops:
  8.9 44.5 %all-gather.2.cloned.1.call-done = bf16[1,24,64,576]{3,1,0,2:T(8,128)(2,1)} async-done(((bf16[1,24,4,576]{3,1,0,2:T(8,128)(2,1)}), bf16[1,24,64,576]{3,1,0,2:T(8,128)(2,1)}) %all-gather.2.cloned.1.call-update) | async-done | bytes 1769488 | tf_op jit(solution)/shard_map/all_gather | solution.py:61
  53.4 1.9 copy.40
  55.3 3.2 %fusion.46 = (f32[1536]{0:T(1024)S(1)}, f32[1536,512]{0,1:T(8,128)}) fusion(bf16[1536,576]{1,0:T(8,128)(2,1)S(1)} %bitcast.161, bf16[1,512,576]{1,2,0:T(8,128)(2,1)S(1)} %copy-done, pred[512]{0:T(512)(128)(4,1)S(1)} %add_compare_fusion), kind=kOutput, calls=%fused_computation.81 | convolution fusion | flops 908327424 | bytes 5511680 | tf_op jit(solution)/shard_map/dot_general | solution.py:27
  58.5 2.6 convert_reduce_fusion
  61.4 3.0 %convolution_bitcast_fusion.1 = f32[1,1536,576]{1,2,0:T(8,128)} fusion(bf16[1,512,576]{1,2,0:T(8,128)(2,1)S(1)} %copy-done, f32[1536,512]{0,1:T(8,128)S(1)} %copy-done.1, f32[1536]{0:T(1024)S(1)} %get-tuple-element.49, pred[512]{0:T(512)(128)(4,1)S(1)} %add_compare_fusion), kind=kOutput, calls=%fused_computation.12 | convolution fusion | flops 908328960 | bytes 7281152 | tf_op jit(solution)/shard_map/dot_general | solution.py:35
  65.0 3.5 %all-to-all-start.1 = ((f32[1,1,24,64]{2,1,0,3:T(1,128)}), f32[1,1,24,64]{2,1,0,3:T(1,128)S(1)}, u32[]{:S(2)}, u32[]{:S(2)}) async-start(f32[1,1,24,64]{2,1,0,3:T(1,128)} %copy.42), calls=%async_computation.1 | async-start | bytes 65536 | tf_op jit(solution)/shard_map/all_to_all | solution.py:80
  68.5 3.8 %slice.8 = f32[1,1536,512]{1,2,0:T(8,128)} slice(f32[1,1536,576]{1,2,0:T(8,128)} %convolution_bitcast_fusion.1), slice={[0:1], [0:1536], [0:512]} | slice | bytes 6291456 | tf_op jit(solution)/shard_map/slice | solution.py:39
  72.3 3.5 %copy.41 = f32[1,1536,512]{2,1,0:T(8,128)} copy(f32[1,1536,512]{1,2,0:T(8,128)} %slice.8) | data formatting | bytes 6291456 | tf_op jit(solution)/shard_map/slice | solution.py:39
  77.6 1.7 fusion.32
  81.0 1.7 fusion.30
  87.8 1.7 fusion.26
  91.2 1.7 fusion.24
  94.6 1.7 fusion.22
  98.0 1.7 fusion.20
  99.7 1.7 fusion.19
  102.2 6.0 %all-to-all-start.2 = ((f32[1,1,24,64]{2,1,0,3:T(1,128)}), f32[1,1,24,64]{2,1,0,3:T(1,128)S(1)}, u32[]{:S(2)}, u32[]{:S(2)}) async-start(f32[1,1,24,64]{2,1,0,3:T(1,128)} %copy.47), calls=%async_computation.2 | async-start | bytes 65536 | tf_op jit(solution)/shard_map/all_to_all | solution.py:81
  108.2 1.7 fusion.18
  110.0 4.9 %all-to-all-done.2 = f32[1,1,24,64]{2,1,0,3:T(1,128)S(1)} async-done(((f32[1,1,24,64]{2,1,0,3:T(1,128)}), f32[1,1,24,64]{2,1,0,3:T(1,128)S(1)}, u32[]{:S(2)}, u32[]{:S(2)}) %all-to-all-start.2) | async-done | bytes 6176 | tf_op jit(solution)/shard_map/all_to_all | solution.py:81
  114.8 4.5 %all-to-all-start = ((f32[16,1,1,24,4,512]{5,4,3,2,1,0:T(4,128)}), f32[16,1,1,24,4,512]{5,4,3,2,1,0:T(4,128)}, u32[]{:S(2)}, u32[]{:S(2)}) async-start(f32[16,1,1,24,4,512]{5,4,3,2,1,0:T(4,128)} %fusion.18), calls=%async_computation | async-start | bytes 6291456 | tf_op jit(solution)/shard_map/all_to_all | solution.py:71
  119.5 5.8 %while.11 = (s32[]{:T(128)}, f32[1,24,24]{2,1,0:T(8,128)S(1)}, s32[24]{0:T(128)S(1)}, s32[]{:T(128)}) while((s32[]{:T(128)}, f32[1,24,24]{2,1,0:T(8,128)S(1)}, s32[24]{0:T(128)S(1)}, s32[]{:T(128)}) %tuple.32), condition=%wide.region_4.5_spmd.clone, body=%wide.region_3.4_spmd.clone.sunk | while | flops 169346 | bytes 9365 | solution.py:22
  126.6 52.0 %all-to-all-done = f32[16,1,1,24,4,512]{5,4,3,2,1,0:T(4,128)} async-done(((f32[16,1,1,24,4,512]{5,4,3,2,1,0:T(4,128)}), f32[16,1,1,24,4,512]{5,4,3,2,1,0:T(4,128)}, u32[]{:S(2)}, u32[]{:S(2)}) %all-to-all-start) | async-done | bytes 3145760 | tf_op jit(solution)/shard_map/all_to_all | solution.py:71
  178.6 2.3 fusion.11
  181.3 7.8 %convolution_bitcast_fusion = f32[7168,24]{1,0:T(8,128)} fusion(bf16[512,7168]{1,0:T(8,128)(2,1)} %param.15, bf16[3,8,4,128]{3,2,1,0:T(4,128)(2,1)S(1)} %bitcast.168), kind=kOutput, calls=%fused_computation.11 | convolution fusion | flops 176160768 | bytes 8052736
  189.2 79.4 %reduce-scatter.4.cloned.1.call-done = f32[448,24]{1,0:T(8,128)} async-done(((f32[7168,24]{1,0:T(8,128)}), f32[448,24]{1,0:T(8,128)}) %reduce-scatter.4.cloned.1.call-update) | async-done | bytes 43024
  (103 shorter events, 25.4 us)
Async XLA Ops:
  6.5 48.7 %copy-start = (bf16[1,512,576]{1,2,0:T(8,128)(2,1)S(1)}, bf16[1,512,576]{1,2,0:T(8,128)(2,1)}, u32[]{:S(2)}) copy-start(bf16[1,512,576]{1,2,0:T(8,128)(2,1)} %param.10) | copy-start | bytes 1769476
  6.5 46.9 %all-gather.2.cloned.1.call-start = ((), (), s32[]{:S(2)}) async-start(), calls=%async_computation.4 | async-start | bytes 2088960 | tf_op jit(solution)/shard_map/all_gather | solution.py:61
  58.5 2.8 %copy-start.1 = (f32[1536,512]{0,1:T(8,128)S(1)}, f32[1536,512]{0,1:T(8,128)}, u32[]{:S(2)}) copy-start(f32[1536,512]{0,1:T(8,128)} %get-tuple-element.50) | copy-start | bytes 9437188
  65.0 37.2 %all-to-all-start.1 = ((f32[1,1,24,64]{2,1,0,3:T(1,128)}), f32[1,1,24,64]{2,1,0,3:T(1,128)S(1)}, u32[]{:S(2)}, u32[]{:S(2)}) async-start(f32[1,1,24,64]{2,1,0,3:T(1,128)} %copy.42), calls=%async_computation.1 | async-start | bytes 65536 | tf_op jit(solution)/shard_map/all_to_all | solution.py:80
  102.2 12.6 %all-to-all-start.2 = ((f32[1,1,24,64]{2,1,0,3:T(1,128)}), f32[1,1,24,64]{2,1,0,3:T(1,128)S(1)}, u32[]{:S(2)}, u32[]{:S(2)}) async-start(f32[1,1,24,64]{2,1,0,3:T(1,128)} %copy.47), calls=%async_computation.2 | async-start | bytes 65536 | tf_op jit(solution)/shard_map/all_to_all | solution.py:81
  109.9 9.4 %copy-start.3 = (bf16[1,24,4,576]{3,2,1,0:T(4,128)(2,1)S(1)}, bf16[1,24,4,576]{3,2,1,0:T(4,128)(2,1)}, u32[]{:S(2)}) copy-start(bf16[1,24,4,576]{3,2,1,0:T(4,128)(2,1)} %param.9) | copy-start | bytes 331780
  109.9 9.5 %copy-start.5 = (s32[1,24]{1,0:T(1,128)S(1)}, s32[1,24]{1,0:T(1,128)}, u32[]{:S(2)}) copy-start(s32[1,24]{1,0:T(1,128)} %param.13) | copy-start | bytes 292
  110.0 15.5 %copy-start.4 = (bf16[1,24,576]{2,1,0:T(8,128)(2,1)S(1)}, bf16[1,24,576]{2,1,0:T(8,128)(2,1)}, u32[]{:S(2)}) copy-start(bf16[1,24,576]{2,1,0:T(8,128)(2,1)} %param.11) | copy-start | bytes 82948
  114.8 63.7 %all-to-all-start = ((f32[16,1,1,24,4,512]{5,4,3,2,1,0:T(4,128)}), f32[16,1,1,24,4,512]{5,4,3,2,1,0:T(4,128)}, u32[]{:S(2)}, u32[]{:S(2)}) async-start(f32[16,1,1,24,4,512]{5,4,3,2,1,0:T(4,128)} %fusion.18), calls=%async_computation | async-start | bytes 6291456 | tf_op jit(solution)/shard_map/all_to_all | solution.py:71
  119.3 149.3 %reduce-scatter.4.cloned.1.call-start = ((), (), s32[]{:S(2)}) async-start(), calls=%async_computation.5 | async-start | bytes 3899392
  119.5 61.7 %copy-start.2 = (bf16[4,512,128]{2,1,0:T(8,128)(2,1)S(1)}, bf16[4,512,128]{2,1,0:T(8,128)(2,1)}, u32[]{:S(2)}) copy-start(bf16[4,512,128]{2,1,0:T(8,128)(2,1)} %param.14) | copy-start | bytes 1572868
Sparse Core Ops, SparseCore 0:
  9.6 43.7 all-gather.1
  189.3 79.2 reduce-scatter.3
